TPU v7x, 128 devices: a whole 4x4x4 slice. The times are simulated.
128 devices in a mesh: section: 2 (over z_lo), patch: 4 (over y), shard: 16 (over z_hi, x, core).
Axes of the slice: x: 4, y: 4, z: 4 (z_hi: 2, z_lo: 2; z = z_hi * 2 + z_lo), core: 2. Of those that a mesh axis runs over, the one named last changes fastest.
Arguments:
- hidden: bfloat16 [32, 1024, 2432], P('shard', 'patch'), may hold values from -6 to 6
- text_kv: bfloat16 [2, 32, 154, 2432], P('section', 'shard'), may hold values from -6 to 6, as said below
- stale_kv: bfloat16 [2, 32, 1024, 2432], P('section', 'shard', 'patch'), may hold values from -6 to 6, as said below
- modulation: float32 [2, 32, 3, 2432], P('section', 'shard'), may hold values from -3 to 3
- score_gain: float32 [2, 64], P('section'), may hold values from 1.5 to 4
- qkv_weight: bfloat16 [2, 2432, 3648], P('section', 'shard'), may hold values from -0.125 to 0.125
- out_weight: bfloat16 [2, 1216, 2432], P('section', None, 'shard'), may hold values from -0.15625 to 0.15625
- final_mod: float32 [32, 2, 2432], P('shard'), may hold values from -3 to 3
- final_weight: bfloat16 [2432, 64], replicated, may hold values from -0.125 to 0.125
- latent: float32 [32, 1024, 64], P('shard', ('patch', 'section')), may hold values from -6 to 6
- step_index: int32 [32], P('shard'), may hold values from 0 to 27
Outputs:
- new_kv: bfloat16 [2, 32, 1024, 2432], P('section', 'shard', 'patch')
- latent_next: float32 [32, 1024, 64], P('shard', ('patch', 'section'))
- denoised: float32 [32, 1024, 64], P('shard', ('patch', 'section'))
Inputs may be any that keep to these rules, and one draw needn't show every extreme that they name: `text_kv`: in every row the first 1216 columns are 19 heads of 64 key features, each head with mean square one up to bfloat16 rounding. `stale_kv`: in every row the first 1216 columns are 19 heads of 64 key features, each head with mean square one up to bfloat16 rounding.
All inputs are finite; a program needn't handle non-finite values.
Results may differ from a plain program's by a relative error of at most 0.008.
Values may be sent and summed in bfloat16 or wider, within the bound.
No kernel may reach another device: no remote copies, remote signals or barrier semaphores. Data moves between devices by JAX's collectives and lax.ppermute only.
A program may use at most 192 MiB of HBM per device.

v0:
```python
import math
import jax
import jax.numpy as jnp
from jax import lax
from jax.sharding import PartitionSpec as P

HEAD = 64
NSTEPS = 28
eps_norm = 1e-06
flow_shift = 3.0


def passed_along(value, axis, steps):
    count = lax.axis_size(axis)
    first, last = (max(0, -steps), min(count, count - steps))
    return lax.ppermute(value, axis, [(source, source + steps) for source in range(first, last)])


def spread(array, axis, root):
    mine = lax.axis_index(axis) == root
    return lax.psum(jnp.where(mine, array, jnp.zeros_like(array)), axis)


def sigma_of(step):
    s = 1.0 - step.astype(jnp.float32) / NSTEPS
    return flow_shift * s / (1.0 + (flow_shift - 1.0) * s)


def modulated(xf, shift, scale):
    mean = jnp.mean(xf, -1, keepdims=True)
    cent = xf - mean
    var = jnp.mean(cent * cent, -1, keepdims=True)
    return cent * lax.rsqrt(var + eps_norm) * (1.0 + scale) + shift


def attend_one(query, keys_all, width, heads):
    count = keys_all.shape[0]
    keys = keys_all[:, :width].reshape(count, heads, HEAD)
    values = keys_all[:, width:].reshape(count, heads, HEAD)
    scores = jnp.einsum("qhe,khe->hqk", query, keys, preferred_element_type=jnp.float32)
    expo = jnp.exp(scores)
    total = jnp.sum(expo, -1)
    weights = expo.astype(jnp.bfloat16)
    mixed = jnp.einsum("hqk,khe->qhe", weights, values, preferred_element_type=jnp.float32)
    mixed = mixed / jnp.transpose(total)[:, :, None]
    return mixed.reshape(query.shape[0], width).astype(jnp.bfloat16)


def run_layer(x, stale_all, text_one, mod_one, gain, w_qkv, w_out, patch_index):
    requests, rows = (x.shape[0], x.shape[1])
    width = w_out.shape[0]
    heads = width // HEAD
    xf = x.astype(jnp.float32)
    normed = modulated(xf, mod_one[:, 0:1, :], mod_one[:, 1:2, :]).astype(jnp.bfloat16)
    proj_in = jnp.einsum("rid,dc->ric", normed, w_qkv, preferred_element_type=jnp.float32)
    q = proj_in[..., :width].reshape(requests, rows, heads, HEAD)
    k = proj_in[..., width : 2 * width].reshape(requests, rows, heads, HEAD)
    v = proj_in[..., 2 * width :]
    q_hat = q * lax.rsqrt(jnp.mean(q * q, -1, keepdims=True) + eps_norm)
    k_hat = k * lax.rsqrt(jnp.mean(k * k, -1, keepdims=True) + eps_norm)
    fresh = jnp.concatenate(
        [k_hat.reshape(requests, rows, width).astype(jnp.bfloat16), v.astype(jnp.bfloat16)], -1
    )
    query = (q_hat * gain / math.sqrt(HEAD)).astype(jnp.bfloat16)
    mixed = lax.dynamic_update_slice_in_dim(stale_all, fresh, patch_index * rows, 1)
    keys_all = jnp.concatenate([text_one, mixed], 1)

    def per_request(pair):
        return attend_one(pair[0], pair[1], width, heads)

    attn = lax.map(per_request, (query, keys_all))
    proj = jnp.einsum("riw,wd->rid", attn, w_out, preferred_element_type=jnp.float32)
    x_next = (xf + mod_one[:, 2:3, :] * proj).astype(jnp.bfloat16)
    return (x_next, fresh)


def on_device(
    hidden,
    text_kv,
    stale_kv,
    modulation,
    score_gain,
    qkv_weight,
    out_weight,
    final_mod,
    final_weight,
    latent,
    step_index,
):
    w_qkv, w_out = (
        lax.all_gather(qkv_weight[0], "shard", axis=0, tiled=True),
        lax.all_gather(out_weight[0], "shard", axis=1, tiled=True),
    )
    stale_all = lax.all_gather(stale_kv[0], "patch", axis=1, tiled=True)
    section = lax.axis_index("section")
    patch_index = lax.axis_index("patch")

    def compute(x):
        return run_layer(
            x, stale_all, text_kv[0], modulation[0], score_gain[0], w_qkv, w_out, patch_index
        )

    def passing(x):
        return (x, jnp.zeros(stale_kv.shape[1:], jnp.bfloat16))

    first, fresh_first = lax.cond(section == 0, compute, passing, hidden)
    arrived = passed_along(first, "section", 1)
    last, fresh_last = lax.cond(section == 1, compute, passing, arrived)
    fresh = jnp.where(section == 0, fresh_first, fresh_last)
    final = modulated(last.astype(jnp.float32), final_mod[:, 0:1, :], final_mod[:, 1:2, :]).astype(
        jnp.bfloat16
    )
    velocity = jnp.einsum("rid,dc->ric", final, final_weight, preferred_element_type=jnp.float32)
    half = latent.shape[1]
    shared = spread(velocity.astype(jnp.bfloat16), "section", 1).astype(velocity.dtype)
    velocity_mine = lax.dynamic_slice_in_dim(shared, section * half, half, 1)
    sig = sigma_of(step_index)[:, None, None]
    sig_next = sigma_of(step_index + 1)[:, None, None]
    latent_next = latent + (sig_next - sig) * velocity_mine
    denoised = latent - sig * velocity_mine
    return (fresh[None], latent_next, denoised)


def solution(mesh):
    in_specs = (
        P("shard", "patch", None),
        P("section", "shard", None, None),
        P("section", "shard", "patch", None),
        P("section", "shard", None, None),
        P("section", None),
        P("section", "shard", None),
        P("section", None, "shard"),
        P("shard", None, None),
        P(),
        P("shard", ("patch", "section"), None),
        P("shard"),
    )
    out_specs = (
        P("section", "shard", "patch", None),
        P("shard", ("patch", "section"), None),
        P("shard", ("patch", "section"), None),
    )
    return jax.shard_map(
        on_device, mesh=mesh, in_specs=in_specs, out_specs=out_specs, check_vma=False
    )
```

profile of v0, /device:TPU:1, one launch (start us, length us, event | category | flops | bytes accessed | tf_op | source)
XLA Modules:
  0.0 642.9 jit_solution(3232019068005679391)
XLA Ops:
  8.0 4.5 copy.28
  13.3 64.7 %all-gather.11.cloned.1.call-done = bf16[1,1216,2432]{1,2,0:T(8,128)(2,1)} async-done(((bf16[1,1216,152]{1,2,0:T(8,128)(2,1)}), bf16[1,1216,2432]{1,2,0:T(8,128)(2,1)}) %all-gather.11.cloned.1.call-update) | async-done | bytes 5914640 | tf_op jit(solution)/shard_map/all_gather | solution.py:92
  78.0 100.0 %all-gather.9.cloned.1.call-done = bf16[1,2,1024,2432]{2,3,1,0:T(8,128)(2,1)} async-done(((bf16[1,2,256,2432]{2,3,1,0:T(8,128)(2,1)}), bf16[1,2,1024,2432]{2,3,1,0:T(8,128)(2,1)}) %all-gather.9.cloned.1.call-update) | async-done | bytes 9961488 | tf_op jit(solution)/shard_map/all_gather | solution.py:94
  177.9 120.4 %all-gather.7.cloned.1.call-done = bf16[1,2432,3648]{2,1,0:T(8,128)(2,1)} async-done(((bf16[1,152,3648]{2,1,0:T(8,128)(2,1)}), bf16[1,2432,3648]{2,1,0:T(8,128)(2,1)}) %all-gather.7.cloned.1.call-update) | async-done | bytes 17743888 | tf_op jit(solution)/shard_map/all_gather | solution.py:91
  298.4 129.6 %conditional.2 = (bf16[2,256,2432]{2,1,0:T(8,128)(2,1)S(1)}, bf16[2,256,2432]{2,1,0:T(8,128)(2,1)}) conditional(s32[]{:T(128)} %convert_element_type.88, bf16[2,256,2432]{2,1,0:T(8,128)(2,1)S(1)} %copy-done.2, (bf16[2,256,2432]{2,1,0:T(8,128)(2,1)S(1)}, f32[1,2,3,2432]{3,1,2,0:T(2,128)S(1)}, bf16[2432,3648]{1,0:T(8,128)(2,1)}, f32[1,64]{1,0:T(1,128)S(1)}, ...), branch_computations={%region_0.0_spmd, %region_1.9_spmd} | conditional | flops 13646128128 | bytes 220811024 | solution.py:106
  300.2 16.5 %fusion.6 = f32[2,256,3648]{1,2,0:T(8,128)} fusion(bf16[2432,3648]{1,0:T(8,128)(2,1)} %get-tuple-element.139, bf16[2,256,2432]{2,1,0:T(8,128)(2,1)S(1)} %get-tuple-element.71, f32[2,2432]{1,0:T(2,128)S(1)} %get-tuple-element.182, f32[2,2432]{1,0:T(2,128)S(1)} %get-tuple-element.183, f32[2,256]{1,0:T(2,128)S(1)} %add_rsqrt_fusion.2, ...), kind=kOutput, calls=%fused_computation.11 | convolution fusion | flops 9092333568 | bytes 27748352 | tf_op jit(solution)/shard_map/cond/branch_1_fun/rid,dc->ric/dot_general | solution.py:55
  316.7 3.3 slice_multiply_fusion
  320.1 2.0 reduce_sum.99
  322.1 4.7 fusion.76
  326.7 2.9 slice.91
  329.6 8.8 %copy.62 = bf16[2,1024,2432]{1,2,0:T(8,128)(2,1)} copy(bf16[2,1024,2432]{1,2,0:T(8,128)(2,1)} %get-tuple-element.74) | data formatting | bytes 19922944 | tf_op jit(solution)/shard_map/cond
  338.4 4.3 pad_maximum_fusion.1
  342.7 5.8 copy.30
  348.5 13.1 %pad_maximum_fusion = bf16[2,1178,2432]{1,2,0:T(8,128)(2,1)} fusion(bf16[2,1024,2432]{1,2,0:T(8,128)(2,1)} %get-tuple-element.180, bf16[2,154,2432]{1,2,0:T(8,128)(2,1)} %bitcast.147), kind=kLoop, calls=%fused_computation.13 | loop fusion | flops 22919168 | bytes 22919168 | tf_op jit(solution)/shard_map/cond/branch_1_fun/concatenate | solution.py:66
  361.9 1.5 multiply_convert_fusion
  363.5 52.4 %while.18 = (s32[]{:T(128)}, bf16[2,256,1216]{1,2,0:T(8,128)(2,1)}, bf16[2,1178,2432]{1,2,0:T(8,128)(2,1)}, bf16[2,256,19,64]{1,3,2,0:T(8,128)(2,1)}, s32[]{:T(128)}) while((s32[]{:T(128)}, bf16[2,256,1216]{1,2,0:T(8,128)(2,1)}, bf16[2,1178,2432]{1,2,0:T(8,128)(2,1)}, bf16[2,256,19,64]{1,3,2,0:T(8,128)(2,1)}, s32[]{:T(128)}) %tuple.88), condition=%wide.region_8.8_spmd, body=%wide.region_6.7_spmd.sunk | while | flops 1478904064 | bytes 82245984 | solution.py:71
  364.0 3.2 dynamic-slice_bitcast_fusion.5
  368.4 9.7 %exponential_reduce_fusion.5 = (f32[19,256]{1,0:T(8,128)S(1)}, f32[19,256,1178]{1,2,0:T(8,128)}) fusion(bf16[1178,19,64]{0,2,1:T(8,128)(2,1)S(1)} %bitcast.134, bf16[2,256,19,64]{1,3,2,0:T(8,128)(2,1)S(1)} %copy-done.5, s32[]{:T(128)} %get-tuple-element.287), kind=kOutput, calls=%fused_computation.clone.1 | convolution fusion | flops 739138304 | bytes 26674180 | tf_op jit(solution)/shard_map/cond/branch_1_fun/while/body/eval_jaxpr/qhe,khe->hqk/dot_general | solution.py:40
  378.1 10.9 %divide_convert_fusion.5 = bf16[256,19,64]{0,2,1:T(8,128)(2,1)S(1)} fusion(bf16[1178,19,64]{0,2,1:T(8,128)(2,1)S(1)} %bitcast.136, f32[19,256,1178]{1,2,0:T(8,128)} %get-tuple-element.265, f32[256,19]{0,1:T(8,128)S(1)} %bitcast.150), kind=kOutput, calls=%fused_computation.5.clone.1 | convolution fusion | flops 739765760 | bytes 26426112 | tf_op jit(solution)/shard_map/cond/branch_1_fun/while/body/eval_jaxpr/hqk,khe->qhe/dot_general | solution.py:44
  389.9 3.2 dynamic-slice_bitcast_fusion.5
  394.4 9.7 %exponential_reduce_fusion.5 = (f32[19,256]{1,0:T(8,128)S(1)}, f32[19,256,1178]{1,2,0:T(8,128)}) fusion(bf16[1178,19,64]{0,2,1:T(8,128)(2,1)S(1)} %bitcast.134, bf16[2,256,19,64]{1,3,2,0:T(8,128)(2,1)S(1)} %copy-done.5, s32[]{:T(128)} %get-tuple-element.287), kind=kOutput, calls=%fused_computation.clone.1 | convolution fusion | flops 739138304 | bytes 26674180 | tf_op jit(solution)/shard_map/cond/branch_1_fun/while/body/eval_jaxpr/qhe,khe->hqk/dot_general | solution.py:40
  404.1 10.9 %divide_convert_fusion.5 = bf16[256,19,64]{0,2,1:T(8,128)(2,1)S(1)} fusion(bf16[1178,19,64]{0,2,1:T(8,128)(2,1)S(1)} %bitcast.136, f32[19,256,1178]{1,2,0:T(8,128)} %get-tuple-element.265, f32[256,19]{0,1:T(8,128)S(1)} %bitcast.150), kind=kOutput, calls=%fused_computation.5.clone.1 | convolution fusion | flops 739765760 | bytes 26426112 | tf_op jit(solution)/shard_map/cond/branch_1_fun/while/body/eval_jaxpr/hqk,khe->qhe/dot_general | solution.py:44
  415.9 7.6 %fusion.19 = bf16[2,256,2432]{2,1,0:T(8,128)(2,1)S(1)} fusion(bf16[2,256,2432]{2,1,0:T(8,128)(2,1)S(1)} %get-tuple-element.71, bf16[2,256,1216]{1,2,0:T(8,128)(2,1)} %get-tuple-element.78, bf16[1216,2432]{0,1:T(8,128)(2,1)} %get-tuple-element.144, f32[2,2432]{1,0:T(2,128)S(1)} %copy-done.10), kind=kOutput, calls=%fused_computation.26 | convolution fusion | flops 3033268224 | bytes 12160000 | tf_op jit(solution)/shard_map/cond/branch_1_fun/riw,wd->rid/dot_general | solution.py:72
  423.5 4.3 copy.46
  428.0 1.5 copy-done.1
  432.2 52.4 %collective-permute-done = bf16[2,256,2432]{2,1,0:T(8,128)(2,1)S(1)} collective-permute-done((bf16[2,256,2432]{2,1,0:T(8,128)(2,1)}, bf16[2,256,2432]{2,1,0:T(8,128)(2,1)S(1)}, u32[]{:S(2)}, u32[]{:S(2)}) %collective-permute-start) | collective-permute-done | bytes 2490400 | tf_op jit(solution)/shard_map/ppermute | solution.py:16
  484.6 4.3 conditional.3
  484.6 1.6 broadcast.161.clone
  490.2 1.8 fusion.69
  492.0 3.4 select_bitcast_fusion
  495.5 138.9 %all-reduce.2.cloned.1.call-done = bf16[2,256,64]{1,2,0:T(8,128)(2,1)} async-done(((bf16[2,256,64]{1,2,0:T(8,128)(2,1)}), bf16[2,256,64]{1,2,0:T(8,128)(2,1)}) %all-reduce.2.cloned.1.call-update) | async-done | bytes 65552 | tf_op jit(solution)/shard_map/psum | solution.py:21
  634.4 1.5 fusion.73
  (60 shorter events, 12.0 us)
Async XLA Ops:
  7.2 483.0 %copy-start = (bf16[2432,64]{0,1:T(8,128)(2,1)S(1)}, bf16[2432,64]{0,1:T(8,128)(2,1)}, u32[]{:S(2)}) copy-start(bf16[2432,64]{0,1:T(8,128)(2,1)} %param.27) | copy-start | bytes 933892
  7.2 70.8 %all-gather.11.cloned.1.call-start = ((), (), s32[]{:S(2)}) async-start(), calls=%async_computation.3 | async-start | bytes 6615040 | tf_op jit(solution)/shard_map/all_gather | solution.py:92
  7.9 290.4 %copy-start.2 = (bf16[2,256,2432]{2,1,0:T(8,128)(2,1)S(1)}, bf16[2,256,2432]{2,1,0:T(8,128)(2,1)}, u32[]{:S(2)}) copy-start(bf16[2,256,2432]{2,1,0:T(8,128)(2,1)} %param.19) | copy-start | bytes 7471108
  7.9 290.4 %copy-start.7 = (f32[1,2,3,2432]{3,1,2,0:T(2,128)S(1)}, f32[1,2,3,2432]{3,1,2,0:T(2,128)}, u32[]{:S(2)}) copy-start(f32[1,2,3,2432]{3,1,2,0:T(2,128)} %param.22) | copy-start | bytes 175108
  7.9 290.4 %copy-start.14 = (f32[1,64]{1,0:T(1,128)S(1)}, f32[1,64]{1,0:T(1,128)}, u32[]{:S(2)}) copy-start(f32[1,64]{1,0:T(1,128)} %param.23) | copy-start | bytes 772
  7.9 170.0 %all-gather.9.cloned.1.call-start = ((), (), s32[]{:S(2)}) async-start(), calls=%async_computation.2 | async-start | bytes 12451840 | tf_op jit(solution)/shard_map/all_gather | solution.py:94
  12.5 285.9 %all-gather.7.cloned.1.call-start = ((), (), s32[]{:S(2)}) async-start(), calls=%async_computation.1 | async-start | bytes 19183616 | tf_op jit(solution)/shard_map/all_gather | solution.py:91
  13.2 621.2 %all-reduce.2.cloned.1.call-start = ((), (), s32[]{:S(2)}) async-start(), calls=%async_computation | async-start | bytes 131072 | tf_op jit(solution)/shard_map/psum | solution.py:21
  298.4 132.5 %copy-start.17 = (s32[2]{0:T(128)S(1)}, s32[2]{0:T(128)}, u32[]{:S(2)}) copy-start(s32[2]{0:T(128)} %param.29) | copy-start | bytes 28
  298.4 133.1 %copy-start.9 = (f32[2,2,2432]{2,1,0:T(2,128)S(1)}, f32[2,2,2432]{2,1,0:T(2,128)}, u32[]{:S(2)}) copy-start(f32[2,2,2432]{2,1,0:T(2,128)} %param.26) | copy-start | bytes 116740
  348.5 13.1 %copy-start.3 = (f32[2,256,1216]{1,2,0:T(8,128)S(1)}, f32[2,256,1216]{1,2,0:T(8,128)}, u32[]{:S(2)}) copy-start(f32[2,256,1216]{1,2,0:T(8,128)} %get-tuple-element.177) | copy-start | bytes 7471108 | tf_op jit(solution)/shard_map/cond
  363.5 52.4 %copy-start.10 = (f32[2,2432]{1,0:T(2,128)S(1)}, f32[2,2432]{1,0:T(2,128)}, u32[]{:S(2)}) copy-start(f32[2,2432]{1,0:T(2,128)} %get-tuple-element.181) | copy-start | bytes 58372 | tf_op jit(solution)/shard_map/cond
  367.1 1.3 copy-start.5
  393.1 1.3 copy-start.5
  428.0 1.5 copy-start.1
  429.4 55.1 %collective-permute-start = (bf16[2,256,2432]{2,1,0:T(8,128)(2,1)}, bf16[2,256,2432]{2,1,0:T(8,128)(2,1)S(1)}, u32[]{:S(2)}, u32[]{:S(2)}) collective-permute-start(bf16[2,256,2432]{2,1,0:T(8,128)(2,1)} %copy-done.1), channel_id=1, source_target_pairs={{0,64},{1,65},{2,66},{3,67},{4,68},{5,69},{6,70},{7,71},{8,72},{9,... | collective-permute-start | bytes 7471112 | tf_op jit(solution)/shard_map/ppermute | solution.py:16
  488.9 1.2 copy-start.12
  488.9 1.2 copy-start.13
  492.0 142.4 %copy-start.8 = (f32[2,128,64]{1,2,0:T(8,128)S(1)}, f32[2,128,64]{1,2,0:T(8,128)}, u32[]{:S(2)}) copy-start(f32[2,128,64]{1,2,0:T(8,128)} %param.28) | copy-start | bytes 196612
  492.0 142.4 %copy-start.15 = (f32[2]{0:T(128)S(1)}, f32[2]{0:T(128)}, u32[]{:S(2)}) copy-start(f32[2]{0:T(128)} %get-tuple-element.171) | copy-start | bytes 28
  492.0 142.4 %copy-start.16 = (f32[2]{0:T(128)S(1)}, f32[2]{0:T(128)}, u32[]{:S(2)}) copy-start(f32[2]{0:T(128)} %get-tuple-element.172) | copy-start | bytes 28
Sparse Core Ops, SparseCore 0:
  10.4 67.5 all-gather.10
  80.2 97.6 all-gather.8
  180.5 117.8 all-gather.6
  492.1 142.2 all-reduce.1
where the time goes:
time: 652 us; the launch traced here: 643 us
  waiting for transfers between devices  478 us (73%)
  matrix products  67.2 us (10%)
  local copies, waits for them, and re-layouts  40.7 us (6%)
  other arithmetic  37.8 us (6%)
  between operations  14.4 us (2%)
    psum x1, waiting for transfers between devices, spread(): return lax.psum(jnp.where(mine, array, jnp.zeros_like(array)), axis)  139 us
    all_gather x1, waiting for transfers between devices, on_device(): lax.all_gather(qkv_weight[0], 'shard', axis=0, tiled=True)  120 us
    all_gather x1, waiting for transfers between devices, on_device(): stale_all = lax.all_gather(stale_kv[0], 'patch', axis=1, tiled=True)  100 us
    all_gather x1, waiting for transfers between devices, on_device(): lax.all_gather(out_weight[0], 'shard', axis=1, tiled=True)  64.7 us
    ppermute x1, waiting for transfers between devices, passed_along(): lax.ppermute(value, axis, [(source, source + steps) for source in range(f...  52.4 us
    dot_general x2, matrix products, attend_one(): jnp.einsum('hqk,khe->qhe', weights, values, preferred_element_type=jnp.fl...  21.8 us
    dot_general x2, matrix products, attend_one(): jnp.einsum('qhe,khe->hqk', query, keys, preferred_element_type=jnp.float32)  19.4 us
    dot_general x1, matrix products, run_layer(): jnp.einsum('rid,dc->ric', normed, w_qkv, preferred_element_type=jnp.float32)  16.5 us
  transfers between devices with their start and end apart: 5, of which 5 were waited for; matrix products, arithmetic and copies ran while one was open for 1% of the time, Pallas kernels for 0%

commit v1 on v0

--- a/solution.py
+++ b/solution.py
@@ -8,6 +8,11 @@
 NSTEPS = 28
 eps_norm = 1e-06
 flow_shift = 3.0
+
+
+def all_by_exchange(shard, mesh_axis, along):
+    sent = jnp.stack([shard] * lax.axis_size(mesh_axis))
+    return jnp.concatenate(lax.all_to_all(sent, mesh_axis, 0, 0), axis=along)
 
 
 def passed_along(value, axis, steps):
@@ -88,7 +93,7 @@
     step_index,
 ):
     w_qkv, w_out = (
-        lax.all_gather(qkv_weight[0], "shard", axis=0, tiled=True),
+        all_by_exchange(qkv_weight[0], "shard", 0),
         lax.all_gather(out_weight[0], "shard", axis=1, tiled=True),
     )
     stale_all = lax.all_gather(stale_kv[0], "patch", axis=1, tiled=True)

time: 652 us -> 728 us (1.12)
  waiting for transfers between devices: 478 us -> 536 us
  starting transfers between devices: 1.59 us -> 10.7 us
  local copies, waits for them, and re-layouts: 40.7 us -> 48.2 us
    all_gather x1, waiting for transfers between devices: 64.7 us -> 225 us  [on_device(): lax.all_gather(out_weight[0], 'shard', axis=1, tiled=True)]
    all_gather x1 -> x0, waiting for transfers between devices: 120 us -> none  [on_device(): lax.all_gather(qkv_weight[0], 'shard', axis=0, tiled=True)]
    all_gather x1, waiting for transfers between devices: 100 us -> 117 us  [on_device(): stale_all = lax.all_gather(stale_kv[0], 'patch', axis=1, tiled=True)]
    all_to_all x0 -> x1, starting transfers between devices: none -> 9.13 us  [all_by_exchange(): return jnp.concatenate(lax.all_to_all(sent, mesh_axis, 0, 0), axis=along)]
  transfers between devices with their start and end apart: 5 -> 5, of which waited for: 5 -> 4; matrix products, arithmetic and copies ran while one was open for 1% -> 2% of each run, Pallas kernels for 0% -> 0%
where the time goes in v1:
time: 728 us; the launch traced here: 718 us
  waiting for transfers between devices  536 us (74%)
  matrix products  67.2 us (9%)
  local copies, waits for them, and re-layouts  48.2 us (7%)
  other arithmetic  37.8 us (5%)
  between operations  14.4 us (2%)
  starting transfers between devices  10.7 us (1%)
    all_gather x1, waiting for transfers between devices, on_device(): lax.all_gather(out_weight[0], 'shard', axis=1, tiled=True)  225 us
    psum x1, waiting for transfers between devices, spread(): return lax.psum(jnp.where(mine, array, jnp.zeros_like(array)), axis)  143 us
    all_gather x1, waiting for transfers between devices, on_device(): stale_all = lax.all_gather(stale_kv[0], 'patch', axis=1, tiled=True)  117 us
    ppermute x1, waiting for transfers between devices, passed_along(): lax.ppermute(value, axis, [(source, source + steps) for source in range(f...  50.9 us
    dot_general x2, matrix products, attend_one(): jnp.einsum('hqk,khe->qhe', weights, values, preferred_element_type=jnp.fl...  21.8 us
    dot_general x2, matrix products, attend_one(): jnp.einsum('qhe,khe->hqk', query, keys, preferred_element_type=jnp.float32)  19.4 us
    dot_general x1, matrix products, run_layer(): jnp.einsum('rid,dc->ric', normed, w_qkv, preferred_element_type=jnp.float32)  16.5 us
  transfers between devices with their start and end apart: 5, of which 4 were waited for; matrix products, arithmetic and copies ran while one was open for 2% of the time, Pallas kernels for 0%

profile of v1, /device:TPU:1, one launch (start us, length us, event | category | flops | bytes accessed | tf_op | source)
XLA Modules:
  0.0 717.6 jit_solution(16488259281013142612)
XLA Ops:
  8.5 7.0 stack.3
  15.4 9.1 %all-to-all-start = ((bf16[16,152,3648]{2,1,0:T(8,128)(2,1)}), bf16[16,152,3648]{2,1,0:T(8,128)(2,1)}, u32[]{:S(2)}, u32[]{:S(2)}) async-start(bf16[16,152,3648]{2,1,0:T(8,128)(2,1)} %stack.3), calls=%async_computation | async-start | bytes 36110336 | tf_op jit(solution)/shard_map/all_to_all | solution.py:15
  24.7 4.5 copy.29
  29.2 224.6 %all-gather.7.cloned.1.call-done = bf16[1,1216,2432]{1,2,0:T(8,128)(2,1)} async-done(((bf16[1,1216,152]{1,2,0:T(8,128)(2,1)}), bf16[1,1216,2432]{1,2,0:T(8,128)(2,1)}) %all-gather.7.cloned.1.call-update) | async-done | bytes 5914640 | tf_op jit(solution)/shard_map/all_gather | solution.py:97
  253.8 116.9 %all-gather.5.cloned.1.call-done = bf16[1,2,1024,2432]{2,3,1,0:T(8,128)(2,1)} async-done(((bf16[1,2,256,2432]{2,3,1,0:T(8,128)(2,1)}), bf16[1,2,1024,2432]{2,3,1,0:T(8,128)(2,1)}) %all-gather.5.cloned.1.call-update) | async-done | bytes 9961488 | tf_op jit(solution)/shard_map/all_gather | solution.py:99
  370.7 129.3 %conditional.2 = (bf16[2,256,2432]{2,1,0:T(8,128)(2,1)S(1)}, bf16[2,256,2432]{2,1,0:T(8,128)(2,1)}) conditional(s32[]{:T(128)} %convert_element_type.88, bf16[2,256,2432]{2,1,0:T(8,128)(2,1)S(1)} %copy-done.2, (bf16[2,256,2432]{2,1,0:T(8,128)(2,1)S(1)}, f32[1,2,3,2432]{3,1,2,0:T(2,128)S(1)}, bf16[2432,3648]{1,0:T(8,128)(2,1)}, f32[1,64]{1,0:T(1,128)S(1)}, ...), branch_computations={%region_0.0_spmd, %region_1.9_spmd} | conditional | flops 13646128128 | bytes 220811024 | solution.py:111
  372.6 16.5 %fusion.6 = f32[2,256,3648]{1,2,0:T(8,128)} fusion(bf16[2432,3648]{1,0:T(8,128)(2,1)} %get-tuple-element.139, bf16[2,256,2432]{2,1,0:T(8,128)(2,1)S(1)} %get-tuple-element.71, f32[2,2432]{1,0:T(2,128)S(1)} %get-tuple-element.182, f32[2,2432]{1,0:T(2,128)S(1)} %get-tuple-element.183, f32[2,256]{1,0:T(2,128)S(1)} %add_rsqrt_fusion.2, ...), kind=kOutput, calls=%fused_computation.11 | convolution fusion | flops 9092333568 | bytes 27748352 | tf_op jit(solution)/shard_map/cond/branch_1_fun/rid,dc->ric/dot_general | solution.py:60
  389.1 3.3 slice_multiply_fusion
  392.4 2.0 reduce_sum.99
  394.4 4.7 fusion.76
  399.0 2.9 slice.91
  401.9 8.8 %copy.63 = bf16[2,1024,2432]{1,2,0:T(8,128)(2,1)} copy(bf16[2,1024,2432]{1,2,0:T(8,128)(2,1)} %get-tuple-element.74) | data formatting | bytes 19922944 | tf_op jit(solution)/shard_map/cond
  410.7 4.3 pad_maximum_fusion.1
  415.0 5.8 copy.31
  420.8 13.1 %pad_maximum_fusion = bf16[2,1178,2432]{1,2,0:T(8,128)(2,1)} fusion(bf16[2,1024,2432]{1,2,0:T(8,128)(2,1)} %get-tuple-element.180, bf16[2,154,2432]{1,2,0:T(8,128)(2,1)} %bitcast.148), kind=kLoop, calls=%fused_computation.13 | loop fusion | flops 22919168 | bytes 22919168 | tf_op jit(solution)/shard_map/cond/branch_1_fun/concatenate | solution.py:71
  434.3 1.5 multiply_convert_fusion
  435.8 52.1 %while.18 = (s32[]{:T(128)}, bf16[2,256,1216]{1,2,0:T(8,128)(2,1)}, bf16[2,1178,2432]{1,2,0:T(8,128)(2,1)}, bf16[2,256,19,64]{1,3,2,0:T(8,128)(2,1)}, s32[]{:T(128)}) while((s32[]{:T(128)}, bf16[2,256,1216]{1,2,0:T(8,128)(2,1)}, bf16[2,1178,2432]{1,2,0:T(8,128)(2,1)}, bf16[2,256,19,64]{1,3,2,0:T(8,128)(2,1)}, s32[]{:T(128)}) %tuple.88), condition=%wide.region_8.8_spmd, body=%wide.region_6.7_spmd.sunk | while | flops 1478904064 | bytes 82245984 | solution.py:76
  435.9 3.2 dynamic-slice_bitcast_fusion.5
  440.4 9.7 %exponential_reduce_fusion.5 = (f32[19,256]{1,0:T(8,128)S(1)}, f32[19,256,1178]{1,2,0:T(8,128)}) fusion(bf16[1178,19,64]{0,2,1:T(8,128)(2,1)S(1)} %bitcast.135, bf16[2,256,19,64]{1,3,2,0:T(8,128)(2,1)S(1)} %copy-done.5, s32[]{:T(128)} %get-tuple-element.287), kind=kOutput, calls=%fused_computation.clone.1 | convolution fusion | flops 739138304 | bytes 26674180 | tf_op jit(solution)/shard_map/cond/branch_1_fun/while/body/eval_jaxpr/qhe,khe->hqk/dot_general | solution.py:45
  450.1 10.9 %divide_convert_fusion.5 = bf16[256,19,64]{0,2,1:T(8,128)(2,1)S(1)} fusion(bf16[1178,19,64]{0,2,1:T(8,128)(2,1)S(1)} %bitcast.137, f32[19,256,1178]{1,2,0:T(8,128)} %get-tuple-element.265, f32[256,19]{0,1:T(8,128)S(1)} %bitcast.151), kind=kOutput, calls=%fused_computation.5.clone.1 | convolution fusion | flops 739765760 | bytes 26426112 | tf_op jit(solution)/shard_map/cond/branch_1_fun/while/body/eval_jaxpr/hqk,khe->qhe/dot_general | solution.py:49
  461.9 3.2 dynamic-slice_bitcast_fusion.5
  466.3 9.7 %exponential_reduce_fusion.5 = (f32[19,256]{1,0:T(8,128)S(1)}, f32[19,256,1178]{1,2,0:T(8,128)}) fusion(bf16[1178,19,64]{0,2,1:T(8,128)(2,1)S(1)} %bitcast.135, bf16[2,256,19,64]{1,3,2,0:T(8,128)(2,1)S(1)} %copy-done.5, s32[]{:T(128)} %get-tuple-element.287), kind=kOutput, calls=%fused_computation.clone.1 | convolution fusion | flops 739138304 | bytes 26674180 | tf_op jit(solution)/shard_map/cond/branch_1_fun/while/body/eval_jaxpr/qhe,khe->hqk/dot_general | solution.py:45
  476.0 10.9 %divide_convert_fusion.5 = bf16[256,19,64]{0,2,1:T(8,128)(2,1)S(1)} fusion(bf16[1178,19,64]{0,2,1:T(8,128)(2,1)S(1)} %bitcast.137, f32[19,256,1178]{1,2,0:T(8,128)} %get-tuple-element.265, f32[256,19]{0,1:T(8,128)S(1)} %bitcast.151), kind=kOutput, calls=%fused_computation.5.clone.1 | convolution fusion | flops 739765760 | bytes 26426112 | tf_op jit(solution)/shard_map/cond/branch_1_fun/while/body/eval_jaxpr/hqk,khe->qhe/dot_general | solution.py:49
  487.8 7.6 %fusion.19 = bf16[2,256,2432]{2,1,0:T(8,128)(2,1)S(1)} fusion(bf16[2,256,2432]{2,1,0:T(8,128)(2,1)S(1)} %get-tuple-element.71, bf16[2,256,1216]{1,2,0:T(8,128)(2,1)} %get-tuple-element.78, bf16[1216,2432]{0,1:T(8,128)(2,1)} %get-tuple-element.144, f32[2,2432]{1,0:T(2,128)S(1)} %copy-done.11), kind=kOutput, calls=%fused_computation.26 | convolution fusion | flops 3033268224 | bytes 12160000 | tf_op jit(solution)/shard_map/cond/branch_1_fun/riw,wd->rid/dot_general | solution.py:77
  495.5 4.3 copy.47
  504.2 50.9 %collective-permute-done = bf16[2,256,2432]{2,1,0:T(8,128)(2,1)S(1)} collective-permute-done((bf16[2,256,2432]{2,1,0:T(8,128)(2,1)}, bf16[2,256,2432]{2,1,0:T(8,128)(2,1)S(1)}, u32[]{:S(2)}, u32[]{:S(2)}) %collective-permute-start) | collective-permute-done | bytes 2490400 | tf_op jit(solution)/shard_map/ppermute | solution.py:21
  555.1 4.4 conditional.3
  555.1 1.6 broadcast.162.clone
  560.7 1.8 fusion.69
  562.6 3.4 select_bitcast_fusion
  566.0 143.0 %all-reduce.2.cloned.1.call-done = bf16[2,256,64]{1,2,0:T(8,128)(2,1)} async-done(((bf16[2,256,64]{1,2,0:T(8,128)(2,1)}), bf16[2,256,64]{1,2,0:T(8,128)(2,1)}) %all-reduce.2.cloned.1.call-update) | async-done | bytes 65552 | tf_op jit(solution)/shard_map/psum | solution.py:26
  709.1 1.5 fusion.73
  (62 shorter events, 13.3 us)
Async XLA Ops:
  7.2 553.5 %copy-start = (bf16[2432,64]{0,1:T(8,128)(2,1)S(1)}, bf16[2432,64]{0,1:T(8,128)(2,1)}, u32[]{:S(2)}) copy-start(bf16[2432,64]{0,1:T(8,128)(2,1)} %param.27) | copy-start | bytes 933892
  7.2 1.3 copy-start.7
  7.2 246.6 %all-gather.7.cloned.1.call-start = ((), (), s32[]{:S(2)}) async-start(), calls=%async_computation.3 | async-start | bytes 6615040 | tf_op jit(solution)/shard_map/all_gather | solution.py:97
  15.4 355.2 %all-to-all-start = ((bf16[16,152,3648]{2,1,0:T(8,128)(2,1)}), bf16[16,152,3648]{2,1,0:T(8,128)(2,1)}, u32[]{:S(2)}, u32[]{:S(2)}) async-start(bf16[16,152,3648]{2,1,0:T(8,128)(2,1)} %stack.3), calls=%async_computation | async-start | bytes 36110336 | tf_op jit(solution)/shard_map/all_to_all | solution.py:15
  24.6 346.1 %copy-start.2 = (bf16[2,256,2432]{2,1,0:T(8,128)(2,1)S(1)}, bf16[2,256,2432]{2,1,0:T(8,128)(2,1)}, u32[]{:S(2)}) copy-start(bf16[2,256,2432]{2,1,0:T(8,128)(2,1)} %param.19) | copy-start | bytes 7471108
  24.6 346.1 %copy-start.8 = (f32[1,2,3,2432]{3,1,2,0:T(2,128)S(1)}, f32[1,2,3,2432]{3,1,2,0:T(2,128)}, u32[]{:S(2)}) copy-start(f32[1,2,3,2432]{3,1,2,0:T(2,128)} %param.22) | copy-start | bytes 175108
  24.6 346.1 %copy-start.15 = (f32[1,64]{1,0:T(1,128)S(1)}, f32[1,64]{1,0:T(1,128)}, u32[]{:S(2)}) copy-start(f32[1,64]{1,0:T(1,128)} %param.23) | copy-start | bytes 772
  24.6 346.1 %all-gather.5.cloned.1.call-start = ((), (), s32[]{:S(2)}) async-start(), calls=%async_computation.2 | async-start | bytes 12451840 | tf_op jit(solution)/shard_map/all_gather | solution.py:99
  29.2 679.9 %all-reduce.2.cloned.1.call-start = ((), (), s32[]{:S(2)}) async-start(), calls=%async_computation.1 | async-start | bytes 131072 | tf_op jit(solution)/shard_map/psum | solution.py:26
  370.7 132.2 %copy-start.18 = (s32[2]{0:T(128)S(1)}, s32[2]{0:T(128)}, u32[]{:S(2)}) copy-start(s32[2]{0:T(128)} %param.29) | copy-start | bytes 28
  370.7 132.8 %copy-start.10 = (f32[2,2,2432]{2,1,0:T(2,128)S(1)}, f32[2,2,2432]{2,1,0:T(2,128)}, u32[]{:S(2)}) copy-start(f32[2,2,2432]{2,1,0:T(2,128)} %param.26) | copy-start | bytes 116740
  420.8 13.1 %copy-start.3 = (f32[2,256,1216]{1,2,0:T(8,128)S(1)}, f32[2,256,1216]{1,2,0:T(8,128)}, u32[]{:S(2)}) copy-start(f32[2,256,1216]{1,2,0:T(8,128)} %get-tuple-element.177) | copy-start | bytes 7471108 | tf_op jit(solution)/shard_map/cond
  435.8 52.1 %copy-start.11 = (f32[2,2432]{1,0:T(2,128)S(1)}, f32[2,2432]{1,0:T(2,128)}, u32[]{:S(2)}) copy-start(f32[2,2432]{1,0:T(2,128)} %get-tuple-element.181) | copy-start | bytes 58372 | tf_op jit(solution)/shard_map/cond
  439.1 1.3 copy-start.5
  465.1 1.3 copy-start.5
  500.0 1.5 copy-start.1
  501.5 53.6 %collective-permute-start = (bf16[2,256,2432]{2,1,0:T(8,128)(2,1)}, bf16[2,256,2432]{2,1,0:T(8,128)(2,1)S(1)}, u32[]{:S(2)}, u32[]{:S(2)}) collective-permute-start(bf16[2,256,2432]{2,1,0:T(8,128)(2,1)} %copy-done.1), channel_id=1, source_target_pairs={{0,64},{1,65},{2,66},{3,67},{4,68},{5,69},{6,70},{7,71},{8,72},{9,... | collective-permute-start | bytes 7471112 | tf_op jit(solution)/shard_map/ppermute | solution.py:21
  559.5 1.2 copy-start.13
  559.5 1.2 copy-start.14
  562.6 146.5 %copy-start.9 = (f32[2,128,64]{1,2,0:T(8,128)S(1)}, f32[2,128,64]{1,2,0:T(8,128)}, u32[]{:S(2)}) copy-start(f32[2,128,64]{1,2,0:T(8,128)} %param.28) | copy-start | bytes 196612
  562.6 146.5 %copy-start.16 = (f32[2]{0:T(128)S(1)}, f32[2]{0:T(128)}, u32[]{:S(2)}) copy-start(f32[2]{0:T(128)} %get-tuple-element.171) | copy-start | bytes 28
  562.6 146.5 %copy-start.17 = (f32[2]{0:T(128)S(1)}, f32[2]{0:T(128)}, u32[]{:S(2)}) copy-start(f32[2]{0:T(128)} %get-tuple-element.172) | copy-start | bytes 28
Sparse Core Ops, SparseCore 0:
  10.4 243.3 all-gather.6
  256.0 114.5 all-gather.4
  562.7 146.3 all-reduce.1
